TPU v7x, 128 devices: a whole 4x4x4 slice. The times are simulated.
128 devices in a mesh: req: 16 (over y, x), hid: 8 (over z, core).
Axes of the slice: x: 4, y: 4, z: 4, core: 2. Of those that a mesh axis runs over, the one named last changes fastest.
Arguments:
- tokens: bfloat16 [32, 16, 2, 4096], P('req', 'hid'), may hold values from -6 to 6
- input_gain: float32 [4096], replicated, may hold values from 0.1 to 1.9
- qkv_weight: bfloat16 [4096, 3, 4096], P(None, None, 'hid'), may hold values from -0.09375 to 0.09375
- out_weight: bfloat16 [4096, 4096], P('hid'), may hold values from -0.375 to 0.375
- in_weight: bfloat16 [4096, 16384], P(None, ('req', 'hid')), may hold values from -0.09375 to 0.09375
- down_weight: bfloat16 [16384, 4096], P(('req', 'hid')), may hold values from -0.046875 to 0.046875
- final_gain: float32 [4096], replicated, may hold values from 0.1 to 1.9
- score_weight: bfloat16 [4096], replicated, may hold values from -0.09375 to 0.09375
- prompt_keys: bfloat16 [32, 2048, 4096], P('req', None, 'hid'), may hold values from -260 to 260
- prompt_values: bfloat16 [32, 2048, 4096], P('req', None, 'hid'), may hold values from -6 to 6
- tail_keys: bfloat16 [32, 16, 64, 4096], P('req', None, None, 'hid'), may hold values from -12 to 12
- tail_values: bfloat16 [32, 16, 64, 4096], P('req', None, None, 'hid'), may hold values from -6 to 6
- prompt_lengths: int32 [32], P('req'), may hold values from 1 to 2048
- tail_lengths: int32 [32, 16], P('req'), may hold values from 0 to 64
Outputs:
- next_hidden: bfloat16 [32, 16, 2, 4096], P('req', 'hid')
- sample_scores: float32 [32, 16, 2], P('req', 'hid')
Inputs may be any that keep to these rules, and one draw needn't show every extreme that they name: `prompt_lengths`: a request's prompt occupies positions 0 to its length - 1. `tail_lengths`: a sample's tail occupies positions 0 to its length - 1.
All inputs are finite; a program needn't handle non-finite values.
Results may differ from a plain program's by a relative error of at most 0.017.
Values may be sent and summed in bfloat16 or wider, within the bound.
No kernel may reach another device: no remote copies, remote signals or barrier semaphores. Data moves between devices by JAX's collectives and lax.ppermute only.
A program may use at most 128 MiB of HBM per device.

v0:
```python
import jax
import jax.numpy as jnp
from jax import lax
from jax.sharding import PartitionSpec as P

HEAD_DIM = 256
ROT = 64
very_low = -1e30


def layer_norm(values, gain):
    centre = jnp.mean(values, axis=-1, keepdims=True)
    centred = values - centre
    spread = jnp.mean(centred * centred, axis=-1, keepdims=True)
    return centred * lax.rsqrt(spread + 1e-05) * gain


def rotate(vectors, positions):
    half_rot = ROT // 2
    frequency = 10000.0 ** (-(jnp.arange(half_rot, dtype=jnp.float32) * (2.0 / ROT)))
    angles = positions.astype(jnp.float32)[..., None] * frequency
    cosine = jnp.cos(angles)[..., None, :]
    sine_part = jnp.sin(angles)[..., None, :]
    paired = vectors[..., :ROT].reshape(vectors.shape[:-1] + (half_rot, 2))
    even_part = paired[..., 0]
    odd_part = paired[..., 1]
    turned = jnp.stack(
        [even_part * cosine - odd_part * sine_part, odd_part * cosine + even_part * sine_part],
        axis=-1,
    )
    return jnp.concatenate(
        [turned.reshape(vectors.shape[:-1] + (ROT,)), vectors[..., ROT:]], axis=-1
    )


def shards(
    tokens,
    input_gain,
    qkv_weight,
    out_weight,
    in_weight,
    down_weight,
    final_gain,
    score_weight,
    prompt_keys,
    prompt_values,
    tail_keys,
    tail_values,
    prompt_lengths,
    tail_lengths,
):
    req_dev, samp_dev, fresh, width = tokens.shape
    own_rows = req_dev * samp_dev * fresh
    residual = tokens.astype(jnp.float32).reshape(own_rows, width)
    normed = layer_norm(residual, input_gain).astype(jnp.bfloat16)
    gathered = lax.all_gather(normed, ("req", "hid"), axis=0, tiled=True)
    hidden_units = jax.nn.gelu(
        jnp.dot(gathered, in_weight, preferred_element_type=jnp.float32), approximate=True
    ).astype(jnp.bfloat16)
    slab_rows, triple, slab_cols = qkv_weight.shape
    flat_qkv = qkv_weight.reshape(slab_rows, triple * slab_cols)
    hid_count = lax.axis_size("hid")
    group_rows = own_rows * hid_count
    group_normed = lax.dynamic_slice_in_dim(
        gathered, lax.axis_index("req") * group_rows, group_rows, 0
    )
    mixed_qkv = jnp.dot(group_normed, flat_qkv, preferred_element_type=jnp.float32).astype(
        jnp.bfloat16
    )
    heads_here = slab_cols // HEAD_DIM
    samples = hid_count * samp_dev
    grouped = mixed_qkv.reshape(hid_count, req_dev, samp_dev, fresh, triple, heads_here, HEAD_DIM)
    grouped = jnp.transpose(grouped, (1, 0, 2, 3, 4, 5, 6)).reshape(
        req_dev, samples, fresh, triple, heads_here, HEAD_DIM
    )
    positions = (
        prompt_lengths[:, None, None]
        + tail_lengths[:, :, None]
        + jnp.arange(fresh, dtype=jnp.int32)[None, None, :]
    )
    queries = rotate(grouped[:, :, :, 0].astype(jnp.float32), positions).astype(jnp.bfloat16)
    new_keys = rotate(grouped[:, :, :, 1].astype(jnp.float32), positions).astype(jnp.bfloat16)
    new_values = grouped[:, :, :, 2]
    prompt_len = prompt_keys.shape[1]
    cached_keys = prompt_keys.reshape(req_dev, prompt_len, heads_here, HEAD_DIM)
    cached_values = prompt_values.reshape(req_dev, prompt_len, heads_here, HEAD_DIM)
    prompt_queries = queries.reshape(req_dev, samples * fresh, heads_here, HEAD_DIM)
    score_scale = HEAD_DIM ** (-0.5)
    prompt_scores = (
        jnp.einsum(
            "rqhd,rkhd->rqhk", prompt_queries, cached_keys, preferred_element_type=jnp.float32
        )
        * score_scale
    )
    keeping = (jnp.arange(prompt_len, dtype=jnp.int32)[None, :] < prompt_lengths[:, None])[
        :, None, None, :
    ]
    prompt_scores = jnp.where(keeping, prompt_scores, very_low)
    peaks = jnp.max(prompt_scores, axis=-1)
    prompt_weights = jnp.where(keeping, jnp.exp(prompt_scores - peaks[..., None]), 0.0)
    totals = jnp.sum(prompt_weights, axis=-1)
    accrued = jnp.einsum(
        "rqhk,rkhd->rqhd",
        prompt_weights.astype(jnp.bfloat16),
        cached_values,
        preferred_element_type=jnp.float32,
    )
    peaks = peaks.reshape(req_dev, samples, fresh, heads_here)
    totals = totals.reshape(req_dev, samples, fresh, heads_here)
    accrued = accrued.reshape(req_dev, samples, fresh, heads_here, HEAD_DIM)
    tail_len = tail_keys.shape[2]
    later_keys = tail_keys.reshape(req_dev, samples, tail_len, heads_here, HEAD_DIM)
    later_values = tail_values.reshape(req_dev, samples, tail_len, heads_here, HEAD_DIM)
    tail_scores = (
        jnp.einsum("rsthd,rskhd->rsthk", queries, later_keys, preferred_element_type=jnp.float32)
        * score_scale
    )
    tail_keep = (jnp.arange(tail_len, dtype=jnp.int32)[None, None, :] < tail_lengths[:, :, None])[
        :, :, None, None, :
    ]
    self_scores = (
        jnp.einsum("rsthd,rsuhd->rsthu", queries, new_keys, preferred_element_type=jnp.float32)
        * score_scale
    )
    position_order = jnp.arange(fresh, dtype=jnp.int32)
    self_keep = (position_order[None, :] <= position_order[:, None])[None, None, :, None, :]
    highest = jnp.maximum(peaks, jnp.max(jnp.where(tail_keep, tail_scores, very_low), axis=-1))
    highest = jnp.maximum(highest, jnp.max(jnp.where(self_keep, self_scores, very_low), axis=-1))
    scaling = jnp.exp(peaks - highest)
    tail_weights = jnp.where(tail_keep, jnp.exp(tail_scores - highest[..., None]), 0.0)
    self_weights = jnp.where(self_keep, jnp.exp(self_scores - highest[..., None]), 0.0)
    totals = totals * scaling + jnp.sum(tail_weights, axis=-1) + jnp.sum(self_weights, axis=-1)
    accrued = accrued * scaling[..., None]
    accrued = accrued + jnp.einsum(
        "rsthk,rskhd->rsthd",
        tail_weights.astype(jnp.bfloat16),
        later_values,
        preferred_element_type=jnp.float32,
    )
    accrued = accrued + jnp.einsum(
        "rsthu,rsuhd->rsthd",
        self_weights.astype(jnp.bfloat16),
        new_values,
        preferred_element_type=jnp.float32,
    )
    attended = (accrued / totals[..., None]).astype(jnp.bfloat16)
    attended = attended.reshape(req_dev, hid_count, samp_dev, fresh, heads_here * HEAD_DIM)
    attended_rows = jnp.transpose(attended, (1, 0, 2, 3, 4)).reshape(
        group_rows, heads_here * HEAD_DIM
    )
    mlp_part = lax.psum_scatter(
        jnp.dot(hidden_units, down_weight, preferred_element_type=jnp.float32),
        ("req", "hid"),
        scatter_dimension=0,
        tiled=True,
    )
    projection_part = lax.psum_scatter(
        jnp.dot(attended_rows, out_weight, preferred_element_type=jnp.float32).astype(jnp.bfloat16),
        "hid",
        scatter_dimension=0,
        tiled=True,
    ).astype(jnp.float32)
    branch_sum = mlp_part + projection_part
    final_state = residual + branch_sum
    next_hidden = final_state.astype(jnp.bfloat16).reshape(req_dev, samp_dev, fresh, width)
    sample_scores = jnp.sum(
        layer_norm(final_state, final_gain) * score_weight.astype(jnp.float32), axis=-1
    )
    return (next_hidden, sample_scores.reshape(req_dev, samp_dev, fresh))


def solution(mesh):
    placed = (
        P("req", "hid", None, None),
        P(),
        P(None, None, "hid"),
        P("hid", None),
        P(None, ("req", "hid")),
        P(("req", "hid"), None),
        P(),
        P(),
        P("req", None, "hid"),
        P("req", None, "hid"),
        P("req", None, None, "hid"),
        P("req", None, None, "hid"),
        P("req"),
        P("req", None),
    )
    return jax.shard_map(
        shards,
        mesh=mesh,
        in_specs=placed,
        out_specs=(P("req", "hid", None, None), P("req", "hid", None)),
        check_vma=False,
    )
```

profile of v0, /device:TPU:0, one launch (start us, length us, event | category | flops | bytes accessed | tf_op | source)
XLA Modules:
  0.0 822.6 jit_solution(10335013178201926168)
XLA Ops:
  7.2 0.9 reshape.217
  8.2 1.0 convert_reduce_fusion
  9.2 1.1 multiply_reduce_fusion.2
  10.4 1.4 multiply_convert_fusion
  12.0 16.9 %copy.120 = bf16[4096,3,512]{0,2,1:T(8,128)(2,1)} copy(bf16[4096,3,512]{2,0,1:T(8,128)(2,1)} %param.16) | data formatting | bytes 25165824 | tf_op args[2]
  29.5 55.2 %all-gather.2.cloned.1.call-done = bf16[1024,4096]{1,0:T(8,128)(2,1)} async-done(((bf16[8,4096]{1,0:T(8,128)(2,1)}), bf16[1024,4096]{1,0:T(8,128)(2,1)}) %all-gather.2.cloned.1.call-update) | async-done | bytes 8388624 | tf_op jit(solution)/shard_map/all_gather | solution.py:56
  84.7 8.7 %convolution_convert_fusion.1 = bf16[64,1536]{1,0:T(8,128)(2,1)S(1)} fusion(bf16[4096,1536]{0,1:T(8,128)(2,1)} %bitcast.109, bf16[1024,4096]{1,0:T(8,128)(2,1)} %all-gather.2.cloned.1.call-done, s32[]{:T(128)S(6)} %select_n.27), kind=kOutput, calls=%fused_computation.10 | convolution fusion | flops 805404672 | bytes 13303812 | tf_op jit(solution)/shard_map/dot_general | solution.py:67
  94.4 0.4 maximum_convert_fusion
  94.8 2.0 copy.123
  97.4 0.4 pad_maximum_fusion
  98.4 2.4 select_reduce_fusion
  100.8 1.9 concatenate.16
  102.8 3.6 fusion.85
  107.3 0.3 fusion.39
  107.9 3.0 fusion.21
  111.3 2.0 fusion.29
  113.7 4.1 convolution_convert_fusion
  117.8 14.4 %fusion.54 = f32[1024,4096]{1,0:T(8,128)} fusion(bf16[128,4096]{1,0:T(8,128)(2,1)S(1)} %copy-done, bf16[1024,4096]{1,0:T(8,128)(2,1)} %all-gather.2.cloned.1.call-done, bf16[4096,128]{1,0:T(8,128)(2,1)S(1)} %copy-done.1), kind=kOutput, calls=%fused_computation.42 | convolution fusion | flops 2148663296 | bytes 27262976 | tf_op jit(solution)/shard_map/dot_general | solution.py:152
  132.2 0.7 copy-done.3
  132.9 13.7 %reduce-scatter.5.cloned.1.call-done = bf16[8,4096]{1,0:T(8,128)(2,1)} async-done(((bf16[64,4096]{1,0:T(8,128)(2,1)}), bf16[8,4096]{1,0:T(8,128)(2,1)}) %reduce-scatter.5.cloned.1.call-update) | async-done | bytes 65552 | tf_op jit(solution)/shard_map/reduce_scatter | solution.py:157
  146.6 666.6 %reduce-scatter.3.cloned.1.call-done = f32[8,4096]{1,0:T(8,128)} async-done(((f32[1024,4096]{1,0:T(8,128)}), f32[8,4096]{1,0:T(8,128)}) %reduce-scatter.3.cloned.1.call-update) | async-done | bytes 131088 | tf_op jit(solution)/shard_map/reduce_scatter | solution.py:151
  813.2 1.1 fusion.84
  814.7 0.7 reshape.235
  815.4 0.7 reshape.236
  (71 shorter events, 5.4 us)
Async XLA Ops:
  7.2 110.6 %copy-start = (bf16[128,4096]{1,0:T(8,128)(2,1)S(1)}, bf16[128,4096]{1,0:T(8,128)(2,1)}, u32[]{:S(2)}) copy-start(bf16[128,4096]{1,0:T(8,128)(2,1)} %param.19) | copy-start | bytes 3145732
  7.2 77.5 %all-gather.2.cloned.1.call-start = ((), (), s32[]{:S(2)}) async-start(), calls=%async_computation.2 | async-start | bytes 8454144 | tf_op jit(solution)/shard_map/all_gather | solution.py:56
  11.9 134.7 %reduce-scatter.5.cloned.1.call-start = ((), (), s32[]{:S(2)}) async-start(), calls=%async_computation.4 | async-start | bytes 589824 | tf_op jit(solution)/shard_map/reduce_scatter | solution.py:157
  11.9 17.0 %copy-start.4 = (s32[2,16]{1,0:T(2,128)S(1)}, s32[2,16]{1,0:T(2,128)}, u32[]{:S(2)}) copy-start(s32[2,16]{1,0:T(2,128)} %param.27) | copy-start | bytes 388
  11.9 17.0 %copy-start.5 = (s32[2]{0:T(128)S(1)}, s32[2]{0:T(128)}, u32[]{:S(2)}) copy-start(s32[2]{0:T(128)} %param.26) | copy-start | bytes 28
  113.3 4.5 copy-start.1
  117.8 695.4 %reduce-scatter.3.cloned.1.call-start = ((), (), s32[]{:S(2)}) async-start(), calls=%async_computation.3 | async-start | bytes 16908288 | tf_op jit(solution)/shard_map/reduce_scatter | solution.py:151
  132.2 0.7 copy-start.3
  132.2 682.2 %copy-start.2 = (f32[4096]{0:T(1024)S(1)}, f32[4096]{0:T(1024)}, u32[]{:S(2)}) copy-start(f32[4096]{0:T(1024)} %param.20) | copy-start | bytes 49156
Sparse Core Ops, SparseCore 0:
  12.0 72.6 all-gather.1
  117.9 28.6 reduce-scatter.4
  149.1 664.0 reduce-scatter.2
where the time goes:
time: 823 us
  waiting for transfers between devices  735 us (89%)
  matrix products  38.6 us (5%)
  local copies, waits for them, and re-layouts  26.3 us (3%)
  between operations  14.1 us (2%)
    reduce_scatter x1, waiting for transfers between devices, shards(): lax.psum_scatter(jnp.dot(hidden_units, down_weight, preferred_element_typ...  667 us
    all_gather x1, waiting for transfers between devices, shards(): gathered = lax.all_gather(normed, ('req', 'hid'), axis=0, tiled=True)  55.2 us
    unnamed x13, local copies, waits for them, and re-layouts  17.6 us
  transfers between devices with their start and end apart: 3, of which 3 were waited for; matrix products, arithmetic and copies ran while one was open for 4% of the time, Pallas kernels for 0%

commit v1 on v0

--- a/solution.py
+++ b/solution.py
@@ -53,7 +53,20 @@
     own_rows = req_dev * samp_dev * fresh
     residual = tokens.astype(jnp.float32).reshape(own_rows, width)
     normed = layer_norm(residual, input_gain).astype(jnp.bfloat16)
-    gathered = lax.all_gather(normed, ("req", "hid"), axis=0, tiled=True)
+
+    def extend_samples_all_here(d_out, field_in):
+        outcome_arr = jnp.concatenate(
+            jax.lax.all_to_all(
+                jnp.stack(tuple((field_in for _ in range(jax.lax.axis_size(("req", "hid")))))),
+                axis_name=("req", "hid"),
+                split_axis=0,
+                concat_axis=0,
+            ),
+            axis=d_out,
+        )
+        return outcome_arr
+
+    gathered = extend_samples_all_here(0, normed)
     hidden_units = jax.nn.gelu(
         jnp.dot(gathered, in_weight, preferred_element_type=jnp.float32), approximate=True
     ).astype(jnp.bfloat16)

time: 823 us -> 870 us (1.057)
  waiting for transfers between devices: 735 us -> 767 us
  starting transfers between devices: 0.12 us -> 11.8 us
    all_to_all x0 -> x1, waiting for transfers between devices: none -> 82.5 us  [extend_samples_all_here(): jax.lax.all_to_all(jnp.stack(tuple((field_in for _ in range(jax.lax.axis_...]
    all_gather x1 -> x0, waiting for transfers between devices: 55.2 us -> none  [shards(): gathered = lax.all_gather(normed, ('req', 'hid'), axis=0, tiled=True)]
    all_to_all x0 -> x1, starting transfers between devices: none -> 11.7 us  [extend_samples_all_here(): jax.lax.all_to_all(jnp.stack(tuple((field_in for _ in range(jax.lax.axis_...]
where the time goes in v1:
time: 870 us; the launch traced here: 869 us
  waiting for transfers between devices  767 us (88%)
  matrix products  38.6 us (4%)
  local copies, waits for them, and re-layouts  30.6 us (4%)
  between operations  14.4 us (2%)
  starting transfers between devices  11.8 us (1%)
    reduce_scatter x1, waiting for transfers between devices, shards(): lax.psum_scatter(jnp.dot(hidden_units, down_weight, preferred_element_typ...  667 us
    all_to_all x1, waiting for transfers between devices, extend_samples_all_here(): jax.lax.all_to_all(jnp.stack(tuple((field_in for _ in range(jax.lax.axis_...  82.5 us
    unnamed x13, local copies, waits for them, and re-layouts  17.6 us
  transfers between devices with their start and end apart: 3, of which 3 were waited for; matrix products, arithmetic and copies ran while one was open for 4% of the time, Pallas kernels for 0%

profile of v1, /device:TPU:0, one launch (start us, length us, event | category | flops | bytes accessed | tf_op | source)
XLA Modules:
  0.0 869.5 jit_solution(1073615240594041712)
XLA Ops:
  7.2 0.9 reshape.244
  8.1 1.0 convert_reduce_fusion
  9.1 1.1 multiply_reduce_fusion.2
  10.4 0.8 multiply_convert_fusion
  11.2 4.3 stack.7
  15.4 11.7 %all-to-all-start = ((bf16[128,8,4096]{2,1,0:T(8,128)(2,1)}), bf16[128,8,4096]{2,1,0:T(8,128)(2,1)}, u32[]{:S(2)}, u32[]{:S(2)}) async-start(bf16[128,8,4096]{2,1,0:T(8,128)(2,1)} %stack.7), calls=%async_computation | async-start | bytes 16777216 | tf_op jit(solution)/shard_map/all_to_all | solution.py:59
  27.2 16.9 %copy.120 = bf16[4096,3,512]{0,2,1:T(8,128)(2,1)} copy(bf16[4096,3,512]{2,0,1:T(8,128)(2,1)} %param.16) | data formatting | bytes 25165824 | tf_op args[2]
  44.7 82.5 %all-to-all-done = bf16[128,8,4096]{2,1,0:T(8,128)(2,1)} async-done(((bf16[128,8,4096]{2,1,0:T(8,128)(2,1)}), bf16[128,8,4096]{2,1,0:T(8,128)(2,1)}, u32[]{:S(2)}, u32[]{:S(2)}) %all-to-all-start) | async-done | bytes 8388640 | tf_op jit(solution)/shard_map/all_to_all | solution.py:59
  127.3 8.7 convolution_convert_fusion.1
  137.0 0.4 maximum_convert_fusion
  137.4 2.0 copy.123
  140.9 2.4 select_reduce_fusion
  143.4 1.9 concatenate.16
  145.4 3.6 fusion.91
  150.5 3.0 fusion.21
  153.9 2.0 fusion.29
  156.3 4.0 convolution_convert_fusion
  160.4 14.4 %fusion.54 = f32[1024,4096]{1,0:T(8,128)} fusion(bf16[128,4096]{1,0:T(8,128)(2,1)S(1)} %copy-done, bf16[4096,128]{1,0:T(8,128)(2,1)S(1)} %copy-done.1, bf16[128,8,4096]{2,1,0:T(8,128)(2,1)} %all-to-all-done), kind=kOutput, calls=%fused_computation.42 | convolution fusion | flops 2148663296 | bytes 27262976 | tf_op jit(solution)/shard_map/dot_general | solution.py:165
  174.9 0.7 copy-done.3
  175.6 17.0 %reduce-scatter.5.cloned.1.call-done = bf16[8,4096]{1,0:T(8,128)(2,1)} async-done(((bf16[64,4096]{1,0:T(8,128)(2,1)}), bf16[8,4096]{1,0:T(8,128)(2,1)}) %reduce-scatter.5.cloned.1.call-update) | async-done | bytes 65552 | tf_op jit(solution)/shard_map/reduce_scatter | solution.py:170
  192.5 667.3 %reduce-scatter.3.cloned.1.call-done = f32[8,4096]{1,0:T(8,128)} async-done(((f32[1024,4096]{1,0:T(8,128)}), f32[8,4096]{1,0:T(8,128)}) %reduce-scatter.3.cloned.1.call-update) | async-done | bytes 131088 | tf_op jit(solution)/shard_map/reduce_scatter | solution.py:164
  859.8 1.1 fusion.90
  861.3 0.7 reshape.263
  862.0 0.7 reshape.264
  (71 shorter events, 6.1 us)
Async XLA Ops:
  7.2 153.2 %copy-start = (bf16[128,4096]{1,0:T(8,128)(2,1)S(1)}, bf16[128,4096]{1,0:T(8,128)(2,1)}, u32[]{:S(2)}) copy-start(bf16[128,4096]{1,0:T(8,128)(2,1)} %param.19) | copy-start | bytes 3145732
  15.4 111.8 %all-to-all-start = ((bf16[128,8,4096]{2,1,0:T(8,128)(2,1)}), bf16[128,8,4096]{2,1,0:T(8,128)(2,1)}, u32[]{:S(2)}, u32[]{:S(2)}) async-start(bf16[128,8,4096]{2,1,0:T(8,128)(2,1)} %stack.7), calls=%async_computation | async-start | bytes 16777216 | tf_op jit(solution)/shard_map/all_to_all | solution.py:59
  27.1 165.4 %reduce-scatter.5.cloned.1.call-start = ((), (), s32[]{:S(2)}) async-start(), calls=%async_computation.4 | async-start | bytes 589824 | tf_op jit(solution)/shard_map/reduce_scatter | solution.py:170
  27.2 17.0 %copy-start.4 = (s32[2,16]{1,0:T(2,128)S(1)}, s32[2,16]{1,0:T(2,128)}, u32[]{:S(2)}) copy-start(s32[2,16]{1,0:T(2,128)} %param.27) | copy-start | bytes 388
  27.2 17.0 %copy-start.5 = (s32[2]{0:T(128)S(1)}, s32[2]{0:T(128)}, u32[]{:S(2)}) copy-start(s32[2]{0:T(128)} %param.26) | copy-start | bytes 28
  155.9 4.5 copy-start.1
  160.3 699.4 %reduce-scatter.3.cloned.1.call-start = ((), (), s32[]{:S(2)}) async-start(), calls=%async_computation.3 | async-start | bytes 16908288 | tf_op jit(solution)/shard_map/reduce_scatter | solution.py:164
  174.9 0.7 copy-start.3
  174.9 686.2 %copy-start.2 = (f32[4096]{0:T(1024)S(1)}, f32[4096]{0:T(1024)}, u32[]{:S(2)}) copy-start(f32[4096]{0:T(1024)} %param.20) | copy-start | bytes 49156
Sparse Core Ops, SparseCore 0:
  160.5 32.0 reduce-scatter.4
  195.0 664.7 reduce-scatter.2
